TPU v7x, 128 devices: a whole 4x4x4 slice. The times are simulated.
128 devices in a mesh: src: 8 (over z, core), rcv: 16 (over y, x).
Axes of the slice: x: 4, y: 4, z: 4, core: 2. Of those that a mesh axis runs over, the one named last changes fastest.
Arguments:
- data: bfloat16 [2, 16384, 16384], P(None, 'src', 'rcv'), may hold values from -15 to 15
- observed: int32 [256, 256], P('src', 'rcv'), may hold values 0 or 1
- band_width: int32 [1], replicated, may hold values from 24 to 48
- left_factor: float32 [32, 8, 64, 256], P(None, 'src'), may hold values from -1.5 to 1.5
- right_factor: float32 [6, 16, 64, 256], P(None, 'rcv'), may hold values from -1.5 to 1.5
Outputs:
- left_out: float32 [32, 8, 64, 256], P(None, 'src')
- right_out: float32 [6, 16, 64, 256], P(None, 'rcv')
All inputs are finite; a program needn't handle non-finite values. No bound on the sum of `observed` on one device may be relied on, other than what follows from the above.
Results may differ from a plain program's by a relative error of at most 0.0044.
The roundings to bfloat16 on the way count: a program that leaves them out, or rounds other values in their place, can miss the bound.
Values may be sent and summed in bfloat16 or wider, within the bound.
No kernel may reach another device: no remote copies, remote signals or barrier semaphores. Data moves between devices by JAX's collectives and lax.ppermute only.
A program may use at most 128 MiB of HBM per device.

v0:
```python
import jax
import jax.numpy as jnp
from jax import lax
from jax.sharding import PartitionSpec as P

ITERS = 2
epsilon = 1e-06


def stacked(factor):
    half_width = factor.shape[1] // 2
    turned = jnp.concatenate([-factor[:, half_width:], factor[:, :half_width]], axis=1)
    return jnp.concatenate([factor, turned], axis=0)


def times_t(first, second):
    return lax.dot_general(
        first, second, (((1,), (1,)), ((), ())), preferred_element_type=jnp.float32
    )


def combine(products):
    count = products.shape[0] // 2
    half_width = products.shape[1] // 2
    upper_part = products[:count]
    lower_part = products[count:]
    return jnp.concatenate(
        [
            upper_part[:, :half_width] + lower_part[:, half_width:],
            upper_part[:, half_width:] - lower_part[:, :half_width],
        ],
        axis=1,
    )


def left_sums(own_rows, curvature):
    numerator, denominator = lax.psum(
        (jnp.sum(own_rows * own_rows), jnp.sum(curvature * curvature)), ("src", "rcv")
    )
    return numerator / (denominator + epsilon)


def right_sums(own_rows, curvature):
    numerator, denominator = lax.psum(
        (jnp.sum(own_rows * own_rows), jnp.sum(curvature * curvature)), ("src", "rcv")
    )
    return numerator / (denominator + epsilon)


def per_device(data, observed, band_width, left_factor, right_factor):
    src_index = lax.axis_index("src")
    rcv_index = lax.axis_index("rcv")
    src_count = lax.axis_size("src")
    rcv_count = lax.axis_size("rcv")
    src_blocks, rcv_blocks = observed.shape
    block_edge = data.shape[1] // src_blocks
    offset_slots = right_factor.shape[0]
    factor_width = left_factor.shape[3]
    per_peer = rcv_blocks // rcv_count
    half_slots = offset_slots // 2
    source_rows = src_index * src_blocks + jnp.arange(src_blocks, dtype=jnp.int32)
    destinations = jnp.arange(rcv_count, dtype=jnp.int32)
    group_ids = jnp.arange(per_peer, dtype=jnp.int32)
    wanted = (
        destinations[None, :, None] + source_rows[:, None, None]
    ) % rcv_count + rcv_count * group_ids[None, None, :]
    selector = (
        jnp.arange(rcv_blocks, dtype=jnp.int32)[None, None, None, :] == wanted[..., None]
    ).astype(jnp.bfloat16)
    blocked = data.reshape(2, src_blocks, block_edge, rcv_blocks, block_edge)
    outgoing = jnp.einsum(
        "ripjq,idgj->drigpq", blocked, selector, preferred_element_type=jnp.float32
    ).astype(jnp.bfloat16)
    out_flags = jnp.einsum(
        "ij,idgj->dig", observed.astype(jnp.bfloat16), selector, preferred_element_type=jnp.float32
    )
    out_flags = out_flags.astype(jnp.bfloat16).reshape(rcv_count, 1, src_blocks, per_peer, 1, 1)
    arrived, arrived_flags = (
        lax.all_to_all(outgoing, "rcv", split_axis=0, concat_axis=0, tiled=True),
        lax.all_to_all(out_flags, "rcv", split_axis=0, concat_axis=0, tiled=True),
    )
    slot_ids = jnp.arange(offset_slots, dtype=jnp.int32)
    source_key = (
        slot_ids[None, :] - half_slots + (rcv_index + source_rows[:, None]) // rcv_count
    ) % (rcv_count * per_peer)
    source_keys = jnp.arange(rcv_count, dtype=jnp.int32)[:, None] * per_peer + group_ids[None, :]
    chooser = (source_keys[None, None, :, :] == source_key[:, :, None, None]).astype(jnp.bfloat16)
    sheared = jnp.einsum(
        "brigpq,itbg->riptq", arrived, chooser, preferred_element_type=jnp.float32
    ).astype(jnp.bfloat16)
    shear_flags = jnp.einsum(
        "big,itbg->it",
        arrived_flags.reshape(rcv_count, src_blocks, per_peer),
        chooser,
        preferred_element_type=jnp.float32,
    ).astype(jnp.bfloat16)
    per_dest = src_blocks // src_count
    offsets = rcv_count * slot_ids + rcv_index - offset_slots * rcv_count // 2
    shifts = offsets // 2
    targets = jnp.arange(src_count, dtype=jnp.int32)
    row_pick = (targets[:, None] - shifts[None, :]) % src_count
    selector_two = (
        jnp.arange(src_count, dtype=jnp.int32)[None, None, :] == row_pick[:, :, None]
    ).astype(jnp.bfloat16)
    split_rows = sheared.reshape(2, per_dest, src_count, block_edge, offset_slots, block_edge)
    outgoing_two = jnp.einsum(
        "ruvptq,etv->eruptq", split_rows, selector_two, preferred_element_type=jnp.float32
    ).astype(jnp.bfloat16)
    flags_two = jnp.einsum(
        "uvt,etv->eut",
        shear_flags.reshape(per_dest, src_count, offset_slots),
        selector_two,
        preferred_element_type=jnp.float32,
    )
    flags_two = flags_two.astype(jnp.bfloat16).reshape(src_count, 1, per_dest, 1, offset_slots, 1)
    arrived_two, arrived_flags_two = (
        lax.all_to_all(outgoing_two, "src", split_axis=0, concat_axis=0, tiled=True),
        lax.all_to_all(flags_two, "src", split_axis=0, concat_axis=0, tiled=True),
    )
    midpoint_ids = jnp.arange(src_blocks, dtype=jnp.int32)
    mid_key = (midpoint_ids[:, None] + (src_index - shifts[None, :]) // src_count) % src_blocks
    mid_keys = (
        jnp.arange(src_count, dtype=jnp.int32)[:, None] * per_dest
        + jnp.arange(per_dest, dtype=jnp.int32)[None, :]
    )
    chooser_two = (mid_keys[None, None, :, :] == mid_key[:, :, None, None]).astype(jnp.bfloat16)
    tile_rows = src_blocks * block_edge
    tile_cols = offset_slots * block_edge
    target = jnp.einsum(
        "aruptq,mtau->mprtq", arrived_two, chooser_two, preferred_element_type=jnp.float32
    )
    target = target.reshape(tile_rows, 2 * tile_cols)
    weight = jnp.einsum(
        "aut,mtau->mt",
        arrived_flags_two.reshape(src_count, per_dest, offset_slots),
        chooser_two,
        preferred_element_type=jnp.float32,
    )
    weight = weight * (jnp.abs(offsets) <= band_width[0]).astype(jnp.float32)[None, :]

    def masked(field):
        shaped = (
            field.reshape(src_blocks, block_edge, 2, offset_slots, block_edge)
            * weight[:, None, None, :, None]
        )
        return shaped.reshape(tile_rows, 2 * tile_cols)

    left_full = left_factor.reshape(tile_rows, factor_width)
    right_full = right_factor.reshape(tile_cols, factor_width)
    left_b = left_full.astype(jnp.bfloat16)
    right_b = right_full.astype(jnp.bfloat16)
    residual = masked(times_t(left_b, stacked(right_b)) - target)
    left_count = tile_rows // rcv_count
    right_count = tile_cols // src_count
    for iteration in range(ITERS):
        residual_b = residual.astype(jnp.bfloat16)
        stacked_right = stacked(right_b)
        gradient = lax.psum(
            jnp.dot(residual_b, stacked_right, preferred_element_type=jnp.float32), "rcv"
        )
        own_rows = lax.dynamic_slice_in_dim(gradient, rcv_index * left_count, left_count, 0)
        curvature = masked(times_t(gradient.astype(jnp.bfloat16), stacked_right))
        step_size = left_sums(own_rows, curvature)
        left_full = left_full - step_size * gradient
        left_b = left_full.astype(jnp.bfloat16)
        residual = residual - step_size * curvature
        residual_b = residual.astype(jnp.bfloat16)
        products = lax.dot_general(
            residual_b, left_b, (((0,), (0,)), ((), ())), preferred_element_type=jnp.float32
        )
        gradient_r = lax.psum(combine(products), "src")
        own_rows = lax.dynamic_slice_in_dim(gradient_r, src_index * right_count, right_count, 0)
        curvature = masked(times_t(left_b, stacked(gradient_r.astype(jnp.bfloat16))))
        step_size = right_sums(own_rows, curvature)
        right_full = right_full - step_size * gradient_r
        right_b = right_full.astype(jnp.bfloat16)
        residual = residual - step_size * curvature
    return (left_full.reshape(left_factor.shape), right_full.reshape(right_factor.shape))


def solution(mesh):
    return jax.shard_map(
        per_device,
        mesh=mesh,
        in_specs=(
            P(None, "src", "rcv"),
            P("src", "rcv"),
            P(),
            P(None, "src", None, None),
            P(None, "rcv", None, None),
        ),
        out_specs=(P(None, "src", None, None), P(None, "rcv", None, None)),
        check_vma=False,
    )
```

profile of v0, /device:TPU:1, one launch (start us, length us, event | category | flops | bytes accessed | tf_op | source)
XLA Modules:
  0.0 1015.3 jit_solution(1019897243227720866)
XLA Ops:
  9.0 7.6 all-to-all-start.2
  16.6 22.1 %reshape.360 = bf16[2,32,64,16,64]{4,3,2,1,0:T(8,128)(2,1)} reshape(bf16[2,2048,1024]{2,1,0:T(8,128)(2,1)} %param.5) | data formatting | bytes 16777216 | tf_op jit(solution)/shard_map/reshape | solution.py:70
  38.7 11.5 %convert_bitcast_fusion = bf16[16,2,32,1,64,64]{5,0,4,1,2,3:T(8,128)(2,1)} fusion(bf16[2,32,64,16,64]{4,3,2,1,0:T(8,128)(2,1)} %reshape.360, s32[32,16]{1,0:T(8,128)S(1)} %add_select_fusion), kind=kOutput, calls=%fused_computation.5 | convolution fusion | flops 138420224 | bytes 16779264 | tf_op jit(solution)/shard_map/ripjq,idgj->drigpq/dot_general | solution.py:71
  50.2 15.1 %copy.128 = bf16[16,2,32,1,64,64]{5,4,1,2,3,0:T(8,128)(2,1)} copy(bf16[16,2,32,1,64,64]{5,0,4,1,2,3:T(8,128)(2,1)} %convert_bitcast_fusion) | data formatting | bytes 16777216 | tf_op jit(solution)/shard_map/convert_element_type | solution.py:73
  65.3 19.6 %reshape.382 = bf16[16,2,131072]{2,1,0:T(2,128)(2,1)} reshape(bf16[16,1,32,2,64,64]{5,4,3,2,1,0:T(8,128)(2,1)} %bitcast.116) | data formatting | bytes 16777216
  85.0 6.7 all-to-all-start
  93.3 120.0 %all-to-all-done = bf16[16,2,131072]{2,1,0:T(2,128)(2,1)} async-done(((bf16[16,2,131072]{2,1,0:T(2,128)(2,1)}), bf16[16,2,131072]{2,1,0:T(2,128)(2,1)}, u32[]{:S(2)}, u32[]{:S(2)}) %all-to-all-start) | async-done | bytes 8388640 | tf_op jit(solution)/shard_map/all_to_all | solution.py:79
  213.3 7.7 all-to-all-start.3
  221.0 19.4 %reshape.383 = bf16[16,1,32,2,64,64]{5,4,3,2,1,0:T(8,128)(2,1)} reshape(bf16[16,2,131072]{2,1,0:T(2,128)(2,1)} %all-to-all-done) | data formatting | bytes 16777216
  240.4 18.5 %fusion.7 = bf16[32,6,2,64,64]{4,1,3,2,0:T(8,128)(2,1)} fusion(bf16[16,2,32,1,64,64]{5,4,1,2,3,0:T(8,128)(2,1)} %bitcast.115, s32[32,6]{1,0:T(8,128)S(1)} %copy.63), kind=kOutput, calls=%fused_computation.6 | convolution fusion | flops 51907584 | bytes 11535104 | tf_op jit(solution)/shard_map/brigpq,itbg->riptq/dot_general | solution.py:88
  259.0 10.6 %convert_bitcast_fusion.1 = bf16[8,2,4,64,6,64]{5,0,2,3,1,4:T(8,128)(2,1)S(1)} fusion(bf16[2,4,8,64,6,64]{5,4,3,0,2,1:T(8,128)(2,1)} %bitcast.117, s32[8,6]{0,1:T(8,128)S(1)} %add_select_fusion.3), kind=kOutput, calls=%fused_computation.20 | convolution fusion | flops 26739072 | bytes 6291648 | tf_op jit(solution)/shard_map/ruvptq,etv->eruptq/dot_general | solution.py:106
  269.5 6.3 copy.129
  275.8 9.1 reshape.384
  284.9 4.8 all-to-all-start.1
  292.2 6.2 mul.154
  298.5 12.2 %mul.155 = f32[2048,768]{0,1:T(8,128)} reshape(f32[32,64,2,6,64]{1,0,4,3,2:T(8,128)} %mul.154) | data formatting | bytes 12582912 | tf_op jit(solution)/shard_map/mul | solution.py:143
  310.6 16.7 %all-to-all-done.1 = bf16[8,2,98304]{2,1,0:T(2,128)(2,1)} async-done(((bf16[8,2,98304]{2,1,0:T(2,128)(2,1)}), bf16[8,2,98304]{2,1,0:T(2,128)(2,1)}, u32[]{:S(2)}, u32[]{:S(2)}) %all-to-all-start.1) | async-done | bytes 3145760 | tf_op jit(solution)/shard_map/all_to_all | solution.py:117
  327.4 8.8 reshape.385
  336.2 11.2 %fusion.15 = f32[32,64,2,6,64]{4,0,1,2,3:T(8,128)} fusion(bf16[8,2,4,64,6,64]{5,2,3,1,4,0:T(4,128)(2,1)} %bitcast.118, s32[32,6]{0,1:T(8,128)S(1)} %add_select_fusion.4, s32[8,4]{0,1:T(4,128)S(1)} %iota_add_fusion), kind=kOutput, calls=%fused_computation.21 | convolution fusion | flops 100669440 | bytes 9438080 | tf_op jit(solution)/shard_map/aruptq,mtau->mprtq/dot_general | solution.py:129
  347.4 14.2 %copy.70 = f32[32,64,2,6,64]{1,0,4,3,2:T(8,128)} copy(f32[32,64,2,6,64]{4,0,1,2,3:T(8,128)} %fusion.15) | data formatting | bytes 12582912 | tf_op jit(solution)/shard_map/aruptq,mtau->mprtq/transpose | solution.py:129
  361.5 11.8 %reshape.363 = f32[2048,768]{0,1:T(8,128)} reshape(f32[32,64,2,6,64]{1,0,4,3,2:T(8,128)} %copy.70) | data formatting | bytes 12582912 | tf_op jit(solution)/shard_map/reshape | solution.py:132
  373.3 5.6 fusion.10
  379.0 2.7 copy-done
  381.6 2.4 fusion.26
  384.1 87.7 %all-reduce.9.cloned.1.call-done = f32[2048,256]{1,0:T(8,128)} async-done(((f32[2048,256]{1,0:T(8,128)}), f32[2048,256]{1,0:T(8,128)}) %all-reduce.9.cloned.1.call-update) | async-done | bytes 2097168 | tf_op jit(solution)/shard_map/psum | solution.py:158
  471.7 8.6 multiply_reduce_fusion.3
  480.9 65.8 %all-reduce.3 = (f32[]{:T(128)}, f32[]{:T(128)}) all-reduce(f32[]{:T(128)} %multiply_reduce_fusion.7, f32[]{:T(128)} %get-tuple-element.32), channel_id=1, replica_groups=mesh['src'=8,'rcv'=16] {'src','rcv'}, use_global_device_ids=true, to_apply=%region_2.3 | all-reduce | flops 2 | bytes 16 | tf_op jit(solution)/shard_map/psum | solution.py:37
  548.0 1.9 fusion.31
  549.9 5.8 fusion.24
  556.8 54.9 %all-reduce.11.cloned.1.call-done = f32[384,256]{0,1:T(8,128)} async-done(((f32[384,256]{0,1:T(8,128)}), f32[384,256]{0,1:T(8,128)}) %all-reduce.11.cloned.1.call-update) | async-done | bytes 393232 | tf_op jit(solution)/shard_map/psum | solution.py:171
  611.7 1.0 convert_element_type.113
  612.8 7.1 multiply_reduce_fusion.2
  620.6 67.1 %all-reduce.2 = (f32[]{:T(128)}, f32[]{:T(128)}) all-reduce(f32[]{:T(128)} %multiply_reduce_fusion.6, f32[]{:T(128)} %get-tuple-element.34), channel_id=1, replica_groups=mesh['src'=8,'rcv'=16] {'src','rcv'}, use_global_device_ids=true, to_apply=%region_7.8 | all-reduce | flops 2 | bytes 16 | tf_op jit(solution)/shard_map/psum | solution.py:44
  689.8 8.6 multiply_subtract_fusion
  698.4 2.7 copy-done.1
  701.0 3.4 fusion.22
  704.5 85.6 %all-reduce.13.cloned.1.call-done = f32[2048,256]{1,0:T(8,128)} async-done(((f32[2048,256]{1,0:T(8,128)}), f32[2048,256]{1,0:T(8,128)}) %all-reduce.13.cloned.1.call-update) | async-done | bytes 2097168 | tf_op jit(solution)/shard_map/psum | solution.py:158
  790.2 7.8 multiply_reduce_fusion.1
  798.0 1.5 multiply_reduce_fusion.5
  799.5 65.8 %all-reduce.1 = (f32[]{:T(128)}, f32[]{:T(128)}) all-reduce(f32[]{:T(128)} %multiply_reduce_fusion.5, f32[]{:T(128)} %get-tuple-element.36), channel_id=1, replica_groups=mesh['src'=8,'rcv'=16] {'src','rcv'}, use_global_device_ids=true, to_apply=%region_12.13 | all-reduce | flops 2 | bytes 16 | tf_op jit(solution)/shard_map/psum | solution.py:37
  866.7 2.8 multiply_subtract_fusion.3
  869.5 1.8 copy-done.4
  871.3 4.1 fusion.20
  876.3 55.2 %all-reduce.15.cloned.1.call-done = f32[384,256]{0,1:T(8,128)} async-done(((f32[384,256]{0,1:T(8,128)}), f32[384,256]{0,1:T(8,128)}) %all-reduce.15.cloned.1.call-update) | async-done | bytes 393232 | tf_op jit(solution)/shard_map/psum | solution.py:171
  931.5 1.1 convert_element_type.119
  932.6 5.9 multiply_reduce_fusion
  939.2 67.1 %all-reduce = (f32[]{:T(128)}, f32[]{:T(128)}) all-reduce(f32[]{:T(128)} %multiply_reduce_fusion.4, f32[]{:T(128)} %multiply_reduce_fusion), channel_id=1, replica_groups=mesh['src'=8,'rcv'=16] {'src','rcv'}, use_global_device_ids=true, to_apply=%region_17.18 | all-reduce | flops 2 | bytes 16 | tf_op jit(solution)/shard_map/psum | solution.py:44
  1007.6 0.9 copy.78
  (78 shorter events, 10.3 us)
Async XLA Ops:
  9.0 76.0 %all-to-all-start.2 = ((bf16[16,1,32,1,1,1]{2,5,4,3,1,0:T(2,128)(2,1)}), bf16[16,1,32,1,1,1]{2,5,4,3,1,0:T(2,128)(2,1)S(1)}, u32[]{:S(2)}, u32[]{:S(2)}) async-start(bf16[16,1,32,1,1,1]{2,5,4,3,1,0:T(2,128)(2,1)} %copy.71), calls=%async_computation.2 | async-start | bytes 16384 | tf_op jit(solution)/shard_map/all_to_all | solution.py:80
  85.0 128.3 %all-to-all-start = ((bf16[16,2,131072]{2,1,0:T(2,128)(2,1)}), bf16[16,2,131072]{2,1,0:T(2,128)(2,1)}, u32[]{:S(2)}, u32[]{:S(2)}) async-start(bf16[16,2,131072]{2,1,0:T(2,128)(2,1)} %reshape.382), calls=%async_computation | async-start | bytes 16777216 | tf_op jit(solution)/shard_map/all_to_all | solution.py:79
  213.3 71.6 %all-to-all-start.3 = ((bf16[8,1,4,1,6,1]{4,2,5,3,1,0:T(4,128)(2,1)}), bf16[8,1,4,1,6,1]{4,2,5,3,1,0:T(4,128)(2,1)S(1)}, u32[]{:S(2)}, u32[]{:S(2)}) async-start(bf16[8,1,4,1,6,1]{4,2,5,3,1,0:T(4,128)(2,1)} %copy.72), calls=%async_computation.3 | async-start | bytes 16384 | tf_op jit(solution)/shard_map/all_to_all | solution.py:118
  275.8 15.2 %copy-start.12 = (f32[6,1,64,256]{3,2,1,0:T(8,128)S(1)}, f32[6,1,64,256]{3,2,1,0:T(8,128)}, u32[]{:S(2)}) copy-start(f32[6,1,64,256]{3,2,1,0:T(8,128)} %param.9) | copy-start | bytes 1179652
  275.8 15.2 %copy-start.6 = (f32[32,1,64,256]{3,2,1,0:T(8,128)S(1)}, f32[32,1,64,256]{3,2,1,0:T(8,128)}, u32[]{:S(2)}) copy-start(f32[32,1,64,256]{3,2,1,0:T(8,128)} %param.8) | copy-start | bytes 6291460
  284.9 42.5 %all-to-all-start.1 = ((bf16[8,2,98304]{2,1,0:T(2,128)(2,1)}), bf16[8,2,98304]{2,1,0:T(2,128)(2,1)}, u32[]{:S(2)}, u32[]{:S(2)}) async-start(bf16[8,2,98304]{2,1,0:T(2,128)(2,1)} %reshape.384), calls=%async_computation.1 | async-start | bytes 6291456 | tf_op jit(solution)/shard_map/all_to_all | solution.py:117
  289.7 182.0 %all-reduce.9.cloned.1.call-start = ((), (), s32[]{:S(2)}) async-start(), calls=%async_computation.4 | async-start | bytes 4194304 | tf_op jit(solution)/shard_map/psum | solution.py:158
  379.0 2.7 copy-start
  384.0 227.7 %all-reduce.11.cloned.1.call-start = ((), (), s32[]{:S(2)}) async-start(), calls=%async_computation.5 | async-start | bytes 786432 | tf_op jit(solution)/shard_map/psum | solution.py:171
  471.7 8.6 copy-start.2
  549.9 6.7 copy-start.13
  556.5 233.6 %all-reduce.13.cloned.1.call-start = ((), (), s32[]{:S(2)}) async-start(), calls=%async_computation.6 | async-start | bytes 4194304 | tf_op jit(solution)/shard_map/psum | solution.py:158
  556.8 132.2 %copy-start.8 = (f32[384,256]{0,1:T(8,128)}, f32[384,256]{0,1:T(8,128)S(1)}, u32[]{:S(2)}) copy-start(f32[384,256]{0,1:T(8,128)S(1)} %copy.75) | copy-start | bytes 1179652
  612.8 7.1 copy-start.7
  689.0 0.7 copy-start.10
  698.4 2.7 copy-start.1
  704.5 162.2 %copy-start.3 = (f32[2048,256]{1,0:T(8,128)S(1)}, f32[2048,256]{1,0:T(8,128)}, u32[]{:S(2)}) copy-start(f32[2048,256]{1,0:T(8,128)} %all-reduce.9.cloned.1.call-done) | copy-start | bytes 6291460
  704.5 227.0 %all-reduce.15.cloned.1.call-start = ((), (), s32[]{:S(2)}) async-start(), calls=%async_computation.7 | async-start | bytes 786432 | tf_op jit(solution)/shard_map/psum | solution.py:171
  866.6 4.6 copy-start.4
  869.5 6.0 copy-start.5
  875.4 132.1 %copy-start.9 = (f32[384,256]{0,1:T(8,128)S(1)}, f32[384,256]{0,1:T(8,128)}, u32[]{:S(2)}) copy-start(f32[384,256]{0,1:T(8,128)} %copy-done.8) | copy-start | bytes 1179652
  931.5 7.0 copy-start.11
Sparse Core Ops, SparseCore 0:
  384.1 87.5 all-reduce.8
  556.7 54.9 all-reduce.10
  704.6 85.5 all-reduce.12
  876.4 54.9 all-reduce.14
where the time goes:
time: 1020 us
  waiting for transfers between devices  420 us (41%)
  blocking collectives  266 us (26%)
  local copies, waits for them, and re-layouts  155 us (15%)
  matrix products  103 us (10%)
  starting transfers between devices  26.9 us (3%)
  other arithmetic  24.4 us (2%)
  between operations  20.2 us (2%)
    psum x2, waiting for transfers between devices, per_device(): lax.psum(jnp.dot(residual_b, stacked_right, preferred_element_type=jnp.fl...  173 us
    psum x2, blocking collectives, right_sums(): lax.psum((jnp.sum(own_rows * own_rows), jnp.sum(curvature * curvature)),...  134 us
    psum x2, blocking collectives, left_sums(): lax.psum((jnp.sum(own_rows * own_rows), jnp.sum(curvature * curvature)),...  132 us
    all_to_all x1, waiting for transfers between devices, per_device(): lax.all_to_all(outgoing, 'rcv', split_axis=0, concat_axis=0, tiled=True)  120 us
    psum x2, waiting for transfers between devices, per_device(): gradient_r = lax.psum(combine(products), 'src')  110 us
    unnamed x34, local copies, waits for them, and re-layouts  64.3 us
    dot_general x5, matrix products, times_t(): lax.dot_general(first, second, (((1,), (1,)), ((), ())), preferred_elemen...  35 us
    reshape x1, local copies, waits for them, and re-layouts, per_device(): blocked = data.reshape(2, src_blocks, block_edge, rcv_blocks, block_edge)  22.1 us
  transfers between devices with their start and end apart: 8, of which 6 were waited for; matrix products, arithmetic and copies ran while one was open for 15% of the time, Pallas kernels for 0%

commit v1 on v0

--- a/solution.py
+++ b/solution.py
@@ -155,9 +155,9 @@
     for iteration in range(ITERS):
         residual_b = residual.astype(jnp.bfloat16)
         stacked_right = stacked(right_b)
-        gradient = lax.psum(
-            jnp.dot(residual_b, stacked_right, preferred_element_type=jnp.float32), "rcv"
-        )
+        part = jnp.dot(residual_b, stacked_right, preferred_element_type=jnp.float32)
+        parts = lax.all_gather(part, "rcv", axis=0, tiled=False)
+        gradient = parts.sum(axis=0)
         own_rows = lax.dynamic_slice_in_dim(gradient, rcv_index * left_count, left_count, 0)
         curvature = masked(times_t(gradient.astype(jnp.bfloat16), stacked_right))
         step_size = left_sums(own_rows, curvature)

time: 1020 us -> 1300 us (1.27)
  waiting for transfers between devices: 420 us -> 631 us
  other arithmetic: 24.4 us -> 62.7 us
  local copies, waits for them, and re-layouts: 155 us -> 180 us
    all_gather x0 -> x2, waiting for transfers between devices: none -> 389 us  [per_device(): parts = lax.all_gather(part, 'rcv', axis=0, tiled=False)]
    psum x2 -> x0, waiting for transfers between devices: 173 us -> none  [per_device(): lax.psum(jnp.dot(residual_b, stacked_right, preferred_element_type=jnp.fl...]
    mul x0 -> x2, local copies, waits for them, and re-layouts: none -> 25.1 us  [per_device(): residual = residual - step_size * curvature]
    reduce_sum x0 -> x2, other arithmetic: none -> 24.2 us  [per_device(): gradient = parts.sum(axis=0)]
    unnamed x34 -> x52, local copies, waits for them, and re-layouts: 64.3 us -> 62.3 us
  transfers between devices with their start and end apart: 8 -> 8, of which waited for: 6 -> 6; matrix products, arithmetic and copies ran while one was open for 15% -> 12% of each run, Pallas kernels for 0% -> 0%
where the time goes in v1:
time: 1300 us; the launch traced here: 1290 us
  waiting for transfers between devices  631 us (49%)
  blocking collectives  264 us (20%)
  local copies, waits for them, and re-layouts  180 us (14%)
  matrix products  102 us (8%)
  other arithmetic  62.7 us (5%)
  starting transfers between devices  26.9 us (2%)
  between operations  20.4 us (2%)
    all_gather x2, waiting for transfers between devices, per_device(): parts = lax.all_gather(part, 'rcv', axis=0, tiled=False)  389 us
    psum x2, blocking collectives, right_sums(): lax.psum((jnp.sum(own_rows * own_rows), jnp.sum(curvature * curvature)),...  134 us
    psum x2, blocking collectives, left_sums(): lax.psum((jnp.sum(own_rows * own_rows), jnp.sum(curvature * curvature)),...  130 us
    all_to_all x1, waiting for transfers between devices, per_device(): lax.all_to_all(outgoing, 'rcv', split_axis=0, concat_axis=0, tiled=True)  120 us
    psum x2, waiting for transfers between devices, per_device(): gradient_r = lax.psum(combine(products), 'src')  105 us
    unnamed x52, local copies, waits for them, and re-layouts  62.3 us
    dot_general x5, matrix products, times_t(): lax.dot_general(first, second, (((1,), (1,)), ((), ())), preferred_elemen...  34.5 us
  transfers between devices with their start and end apart: 8, of which 6 were waited for; matrix products, arithmetic and copies ran while one was open for 12% of the time, Pallas kernels for 0%

profile of v1, /device:TPU:1, one launch (start us, length us, event | category | flops | bytes accessed | tf_op | source)
XLA Modules:
  0.0 1287.7 jit_solution(17860866169734825036)
XLA Ops:
  9.0 7.6 all-to-all-start.2
  16.6 22.1 %reshape.396 = bf16[2,32,64,16,64]{4,3,2,1,0:T(8,128)(2,1)} reshape(bf16[2,2048,1024]{2,1,0:T(8,128)(2,1)} %param.5) | data formatting | bytes 16777216 | tf_op jit(solution)/shard_map/reshape | solution.py:70
  38.7 11.5 convert_bitcast_fusion
  50.2 15.1 %copy.140 = bf16[16,2,32,1,64,64]{5,4,1,2,3,0:T(8,128)(2,1)} copy(bf16[16,2,32,1,64,64]{5,0,4,1,2,3:T(8,128)(2,1)} %convert_bitcast_fusion) | data formatting | bytes 16777216 | tf_op jit(solution)/shard_map/convert_element_type | solution.py:73
  65.3 19.6 %reshape.423 = bf16[16,2,131072]{2,1,0:T(2,128)(2,1)} reshape(bf16[16,1,32,2,64,64]{5,4,3,2,1,0:T(8,128)(2,1)} %bitcast.139) | data formatting | bytes 16777216
  85.0 6.7 all-to-all-start
  93.3 120.0 %all-to-all-done = bf16[16,2,131072]{2,1,0:T(2,128)(2,1)} async-done(((bf16[16,2,131072]{2,1,0:T(2,128)(2,1)}), bf16[16,2,131072]{2,1,0:T(2,128)(2,1)}, u32[]{:S(2)}, u32[]{:S(2)}) %all-to-all-start) | async-done | bytes 8388640 | tf_op jit(solution)/shard_map/all_to_all | solution.py:79
  213.3 7.7 all-to-all-start.3
  221.0 19.5 %reshape.424 = bf16[16,1,32,2,64,64]{5,4,3,2,1,0:T(8,128)(2,1)} reshape(bf16[16,2,131072]{2,1,0:T(2,128)(2,1)} %all-to-all-done) | data formatting | bytes 16777216
  240.5 18.5 %fusion.7 = bf16[32,6,2,64,64]{4,1,3,2,0:T(8,128)(2,1)} fusion(bf16[16,2,32,1,64,64]{5,4,1,2,3,0:T(8,128)(2,1)} %bitcast.138, s32[32,6]{1,0:T(8,128)S(1)} %copy.67), kind=kOutput, calls=%fused_computation.9 | convolution fusion | flops 51907584 | bytes 11535104 | tf_op jit(solution)/shard_map/brigpq,itbg->riptq/dot_general | solution.py:88
  259.0 10.8 convert_bitcast_fusion.1
  269.8 6.3 copy.141
  276.0 9.1 reshape.425
  285.1 4.8 all-to-all-start.1
  292.7 6.2 mul.183.clone
  298.9 11.9 mul.184
  310.9 16.7 %all-to-all-done.1 = bf16[8,2,98304]{2,1,0:T(2,128)(2,1)} async-done(((bf16[8,2,98304]{2,1,0:T(2,128)(2,1)}), bf16[8,2,98304]{2,1,0:T(2,128)(2,1)}, u32[]{:S(2)}, u32[]{:S(2)}) %all-to-all-start.1) | async-done | bytes 3145760 | tf_op jit(solution)/shard_map/all_to_all | solution.py:117
  327.6 8.8 reshape.426
  336.4 11.2 fusion.15
  347.6 14.2 %copy.74 = f32[32,64,2,6,64]{1,0,4,3,2:T(8,128)} copy(f32[32,64,2,6,64]{4,0,1,2,3:T(8,128)} %fusion.15) | data formatting | bytes 12582912 | tf_op jit(solution)/shard_map/aruptq,mtau->mprtq/transpose | solution.py:129
  361.7 11.8 reshape.399
  373.5 5.6 fusion.10
  379.2 2.6 copy-done
  381.8 2.4 fusion.26
  384.2 195.6 %all-gather.5.cloned.1.call-done = f32[32768,256]{1,0:T(8,128)} async-done(((f32[2048,256]{1,0:T(8,128)}), f32[32768,256]{1,0:T(8,128)}) %all-gather.5.cloned.1.call-update) | async-done | bytes 33554448 | tf_op jit(solution)/shard_map/all_gather | solution.py:159
  579.9 12.1 reduce_sum.90
  591.9 7.8 multiply_reduce_fusion.3
  600.4 65.1 %all-reduce.3 = (f32[]{:T(128)}, f32[]{:T(128)}) all-reduce(f32[]{:T(128)} %multiply_reduce_fusion.7, f32[]{:T(128)} %get-tuple-element.34), channel_id=1, replica_groups=mesh['src'=8,'rcv'=16] {'src','rcv'}, use_global_device_ids=true, to_apply=%region_2.3 | all-reduce | flops 2 | bytes 16 | tf_op jit(solution)/shard_map/psum | solution.py:37
  666.8 3.4 bitcast_subtract_fusion.1
  671.0 4.3 fusion.24
  677.1 3.2 sub.101
  680.3 51.8 %all-reduce.7.cloned.1.call-done = f32[384,256]{0,1:T(8,128)} async-done(((f32[384,256]{0,1:T(8,128)}), f32[384,256]{0,1:T(8,128)}) %all-reduce.7.cloned.1.call-update) | async-done | bytes 393232 | tf_op jit(solution)/shard_map/psum | solution.py:171
  733.4 8.6 multiply_reduce_fusion.1
  742.8 67.1 %all-reduce.2 = (f32[]{:T(128)}, f32[]{:T(128)}) all-reduce(f32[]{:T(128)} %multiply_reduce_fusion.6, f32[]{:T(128)} %get-tuple-element.36), channel_id=1, replica_groups=mesh['src'=8,'rcv'=16] {'src','rcv'}, use_global_device_ids=true, to_apply=%region_7.8 | all-reduce | flops 2 | bytes 16 | tf_op jit(solution)/shard_map/psum | solution.py:44
  811.2 10.1 multiply_multiply_fusion
  821.3 13.3 %copy.80 = f32[32,64,2,6,64]{1,0,4,3,2:T(8,128)} copy(f32[32,64,2,6,64]{4,1,3,2,0:T(8,128)} %multiply_multiply_fusion) | data formatting | bytes 12582912 | tf_op jit(solution)/shard_map/mul | solution.py:177
  834.6 11.8 mul.201
  846.4 8.7 fusion.28
  857.9 2.4 fusion.22
  860.4 193.6 %all-gather.7.cloned.1.call-done = f32[32768,256]{1,0:T(8,128)} async-done(((f32[2048,256]{1,0:T(8,128)}), f32[32768,256]{1,0:T(8,128)}) %all-gather.7.cloned.1.call-update) | async-done | bytes 33554448 | tf_op jit(solution)/shard_map/all_gather | solution.py:159
  1054.0 12.1 reduce_sum.95
  1066.8 7.0 multiply_reduce_fusion.2
  1073.8 65.1 %all-reduce.1 = (f32[]{:T(128)}, f32[]{:T(128)}) all-reduce(f32[]{:T(128)} %multiply_reduce_fusion.5, f32[]{:T(128)} %get-tuple-element.38), channel_id=1, replica_groups=mesh['src'=8,'rcv'=16] {'src','rcv'}, use_global_device_ids=true, to_apply=%region_12.13 | all-reduce | flops 2 | bytes 16 | tf_op jit(solution)/shard_map/psum | solution.py:37
  1140.2 6.4 fusion.20
  1147.6 1.9 sub.107
  1149.6 53.7 %all-reduce.9.cloned.1.call-done = f32[384,256]{0,1:T(8,128)} async-done(((f32[384,256]{0,1:T(8,128)}), f32[384,256]{0,1:T(8,128)}) %all-reduce.9.cloned.1.call-update) | async-done | bytes 393232 | tf_op jit(solution)/shard_map/psum | solution.py:171
  1205.3 5.4 multiply_reduce_fusion
  1211.3 67.1 %all-reduce = (f32[]{:T(128)}, f32[]{:T(128)}) all-reduce(f32[]{:T(128)} %multiply_reduce_fusion.4, f32[]{:T(128)} %multiply_reduce_fusion), channel_id=1, replica_groups=mesh['src'=8,'rcv'=16] {'src','rcv'}, use_global_device_ids=true, to_apply=%region_17.18 | all-reduce | flops 2 | bytes 16 | tf_op jit(solution)/shard_map/psum | solution.py:44
  (108 shorter events, 19.0 us)
Async XLA Ops:
  9.0 76.0 %all-to-all-start.2 = ((bf16[16,1,32,1,1,1]{2,5,4,3,1,0:T(2,128)(2,1)}), bf16[16,1,32,1,1,1]{2,5,4,3,1,0:T(2,128)(2,1)S(1)}, u32[]{:S(2)}, u32[]{:S(2)}) async-start(bf16[16,1,32,1,1,1]{2,5,4,3,1,0:T(2,128)(2,1)} %copy.75), calls=%async_computation.2 | async-start | bytes 16384 | tf_op jit(solution)/shard_map/all_to_all | solution.py:80
  85.0 128.3 %all-to-all-start = ((bf16[16,2,131072]{2,1,0:T(2,128)(2,1)}), bf16[16,2,131072]{2,1,0:T(2,128)(2,1)}, u32[]{:S(2)}, u32[]{:S(2)}) async-start(bf16[16,2,131072]{2,1,0:T(2,128)(2,1)} %reshape.423), calls=%async_computation | async-start | bytes 16777216 | tf_op jit(solution)/shard_map/all_to_all | solution.py:79
  213.3 71.8 %all-to-all-start.3 = ((bf16[8,1,4,1,6,1]{4,2,5,3,1,0:T(4,128)(2,1)}), bf16[8,1,4,1,6,1]{4,2,5,3,1,0:T(4,128)(2,1)S(1)}, u32[]{:S(2)}, u32[]{:S(2)}) async-start(bf16[8,1,4,1,6,1]{4,2,5,3,1,0:T(4,128)(2,1)} %copy.76), calls=%async_computation.3 | async-start | bytes 16384 | tf_op jit(solution)/shard_map/all_to_all | solution.py:118
  276.0 15.3 %copy-start.12 = (f32[6,1,64,256]{3,2,1,0:T(8,128)S(1)}, f32[6,1,64,256]{3,2,1,0:T(8,128)}, u32[]{:S(2)}) copy-start(f32[6,1,64,256]{3,2,1,0:T(8,128)} %param.9) | copy-start | bytes 1179652
  276.0 15.3 %copy-start.4 = (f32[32,1,64,256]{3,2,1,0:T(8,128)S(1)}, f32[32,1,64,256]{3,2,1,0:T(8,128)}, u32[]{:S(2)}) copy-start(f32[32,1,64,256]{3,2,1,0:T(8,128)} %param.8) | copy-start | bytes 6291460
  285.1 42.5 %all-to-all-start.1 = ((bf16[8,2,98304]{2,1,0:T(2,128)(2,1)}), bf16[8,2,98304]{2,1,0:T(2,128)(2,1)}, u32[]{:S(2)}, u32[]{:S(2)}) async-start(bf16[8,2,98304]{2,1,0:T(2,128)(2,1)} %reshape.425), calls=%async_computation.1 | async-start | bytes 6291456 | tf_op jit(solution)/shard_map/all_to_all | solution.py:117
  289.9 290.0 %all-gather.5.cloned.1.call-start = ((), (), s32[]{:S(2)}) async-start(), calls=%async_computation.6 | async-start | bytes 35651584 | tf_op jit(solution)/shard_map/all_gather | solution.py:159
  291.2 0.6 copy-start.20
  291.3 0.6 copy-start.18
  310.8 25.5 %copy-start.19 = (s32[32,6]{0,1:T(8,128)S(1)}, s32[32,6]{0,1:T(8,128)}, u32[]{:S(2)}) copy-start(s32[32,6]{0,1:T(8,128)} %copy-done.18) | copy-start | bytes 2308
  310.9 25.5 %copy-start.21 = (s32[8,4]{0,1:T(4,128)S(1)}, s32[8,4]{0,1:T(4,128)}, u32[]{:S(2)}) copy-start(s32[8,4]{0,1:T(4,128)} %copy-done.20) | copy-start | bytes 388
  379.1 2.6 copy-start
  384.2 347.9 %all-reduce.7.cloned.1.call-start = ((), (), s32[]{:S(2)}) async-start(), calls=%async_computation.4 | async-start | bytes 786432 | tf_op jit(solution)/shard_map/psum | solution.py:171
  666.8 4.2 copy-start.1
  670.3 5.0 copy-start.3
  671.0 5.2 copy-start.13
  671.0 6.1 copy-start.5
  676.1 377.8 %all-gather.7.cloned.1.call-start = ((), (), s32[]{:S(2)}) async-start(), calls=%async_computation.7 | async-start | bytes 35651584 | tf_op jit(solution)/shard_map/all_gather | solution.py:159
  733.4 8.6 copy-start.6
  855.1 2.6 copy-start.2
  856.4 1.4 copy-start.8
  856.5 1.4 copy-start.14
  856.5 1.4 copy-start.16
  860.3 342.9 %all-reduce.9.cloned.1.call-start = ((), (), s32[]{:S(2)}) async-start(), calls=%async_computation.5 | async-start | bytes 786432 | tf_op jit(solution)/shard_map/psum | solution.py:171
  1054.0 12.8 copy-start.9
  1054.0 12.8 copy-start.15
  1054.0 12.8 copy-start.17
  1149.5 61.1 %copy-start.11 = (f32[32,1,64,256]{3,2,1,0:T(8,128)}, f32[32,1,64,256]{3,2,1,0:T(8,128)S(1)}, u32[]{:S(2)}) copy-start(f32[32,1,64,256]{3,2,1,0:T(8,128)S(1)} %sub.107) | copy-start | bytes 6291460
  1205.2 5.4 copy-start.10
  1205.3 74.5 %copy-start.7 = (f32[384,256]{0,1:T(8,128)S(1)}, f32[384,256]{0,1:T(8,128)}, u32[]{:S(2)}) copy-start(f32[384,256]{0,1:T(8,128)} %copy.81) | copy-start | bytes 1179652
Sparse Core Ops, SparseCore 0:
  384.3 195.5 all-gather.4
  676.3 55.7 all-reduce.6
  860.4 193.5 all-gather.6
  1147.6 55.5 all-reduce.8
